TPU v7x, 128 devices: a whole 4x4x4 slice. The times are simulated.
128 devices in a mesh: tile: 32 (over x, y_hi, z), tm: 4 (over y_lo, core).
Axes of the slice: x: 4, y: 4 (y_hi: 2, y_lo: 2; y = y_hi * 2 + y_lo), z: 4, core: 2. Of those that a mesh axis runs over, the one named last changes fastest.
Arguments:
- volume: bfloat16 [16, 256, 16, 128], P('tm', 'tile'), may hold values from -6 to 6
- frame_index: int32 [16], P('tm'), may hold values from 0 to 31, as said below
- tile_offset: int32 [3], replicated, may hold values from 0 to 255
- conv_first: bfloat16 [16, 1, 3, 3, 3], replicated, may hold values from -1.25 to 1.25
- conv_second: bfloat16 [16, 16, 3, 3, 3], replicated, may hold values from -0.3125 to 0.3125
- patch_weight: bfloat16 [8192, 1024], replicated, may hold values from -0.5 to 0.5
- attend_weight: bfloat16 [1024, 3072], P(None, 'tile')
- mixing_weight: bfloat16 [1024, 1024], P(None, 'tile'), may hold values from -0.1875 to 0.1875
- cube_output_projector: bfloat16 [1024, 512], replicated, may hold values from -0.1875 to 0.1875
Outputs:
- prediction_tensor: bfloat16 [16, 32, 2, 16, 512], P('tm', 'tile')
Inputs may be any that keep to these rules, and one draw needn't show every extreme that they name: `frame_index`: strictly increasing; the first frame is 0 and the last is 31.
All inputs are finite; a program needn't handle non-finite values.
Results may differ from a plain program's by a relative error of at most 0.015.
Values may be sent and summed in bfloat16 or wider, within the bound.
No kernel may reach another device: no remote copies, remote signals or barrier semaphores. Data moves between devices by JAX's collectives and lax.ppermute only.
A program may use at most 256 MiB of HBM per device.

v0:
```python
import math
import jax
import jax.numpy as jnp
from jax import lax
from jax.sharding import PartitionSpec as P

CH = 16
D = 1024
HEADS = 8
HD = 128
BLOCK_EDGE_UNITS = 8


def with_halo(cells, sides, width):
    for axis, dim in sides:
        count = lax.axis_size(axis)
        ends = count - 1
        head = lax.slice_in_dim(cells, 0, width, axis=dim)
        tail = lax.slice_in_dim(cells, cells.shape[dim] - width, cells.shape[dim], axis=dim)
        cells = jnp.concatenate(
            [
                lax.ppermute(tail, axis, [(i, (i + 1) % count) for i in range(ends)]),
                cells,
                lax.ppermute(head, axis, [((i + 1) % count, i) for i in range(ends)]),
            ],
            axis=dim,
        )
    return cells


def convolve_strip(field_in, kernel):
    return lax.conv_general_dilated(
        field_in,
        kernel,
        (1, 1, 1),
        ((0, 0), (1, 1), (1, 1)),
        dimension_numbers=("NCDHW", "OIDHW", "NCDHW"),
        preferred_element_type=jnp.float32,
    )


def settle(values_in):
    return values_in * lax.rsqrt(jnp.mean(values_in * values_in, axis=-1, keepdims=True) + 1e-05)


def embed_time(frame_index):
    frequency = jnp.exp(-math.log(1000.0) * jnp.arange(D, dtype=jnp.float32) / D)
    phase_shift = (jnp.arange(D) % 2).astype(jnp.float32) * (math.pi / 2)
    return (jnp.sin(frame_index.astype(jnp.float32)[:, None] * frequency + phase_shift), frequency)


def embed_space(tile_offset, place_x, place_z, place_y, frequency):
    along_x = (tile_offset[0] + BLOCK_EDGE_UNITS * place_x).astype(jnp.float32)
    along_z = (tile_offset[1] + BLOCK_EDGE_UNITS * place_z).astype(jnp.float32)
    along_y = (tile_offset[2] + BLOCK_EDGE_UNITS * place_y).astype(jnp.float32)
    summed = jnp.sin(along_x[:, None, None, None] * frequency) + jnp.sin(
        along_z[None, :, None, None] * frequency + 1.0
    )
    summed = summed + jnp.sin(along_y[None, None, :, None] * frequency + 2.0)
    return summed.reshape(-1, D)


def attend_frames(query, keys_all, values_all, first_frame):
    cube_count = keys_all.shape[1]
    scores = jnp.einsum(
        "tnhd,smhd->htnsm", query, keys_all, preferred_element_type=jnp.float32
    ) / math.sqrt(HD)
    scores = scores.reshape(scores.shape[0], query.shape[0], query.shape[1], -1)
    query_frame = first_frame + jnp.arange(query.shape[0])
    allowed = jnp.arange(keys_all.shape[0])[None, :] <= query_frame[:, None]
    allowed = jnp.repeat(allowed, cube_count, axis=1)
    scores = jnp.where(allowed[None, :, None, :], scores, -1e30)
    shifted = jnp.exp(scores - jnp.max(scores, axis=-1, keepdims=True))
    weights = (shifted / jnp.sum(shifted, axis=-1, keepdims=True)).astype(jnp.bfloat16)
    flat_values = values_all.reshape(-1, values_all.shape[2], values_all.shape[3])
    return jnp.einsum(
        "htnk,khd->tnhd", weights, flat_values, preferred_element_type=jnp.float32
    ).astype(jnp.bfloat16)


def local(
    volume,
    frame_index,
    tile_offset,
    conv_first,
    conv_second,
    patch_weight,
    attend_weight,
    mixing_weight,
    cube_output_projector,
):
    local_frames, width_here, cells_in_depth, height_extent = volume.shape
    tile_place = lax.axis_index("tile")
    padded = with_halo(volume, (("tile", 1),), 1)
    first_maps = jax.nn.silu(convolve_strip(padded[:, None], conv_first)).astype(jnp.bfloat16)
    first_maps = with_halo(first_maps, (("tile", 2),), 1)
    second_maps = jax.nn.silu(convolve_strip(first_maps, conv_second)).astype(jnp.bfloat16)
    stride_along_x = width_here // BLOCK_EDGE_UNITS
    patch_cubes = second_maps.reshape(
        local_frames,
        CH,
        stride_along_x,
        BLOCK_EDGE_UNITS,
        cells_in_depth // BLOCK_EDGE_UNITS,
        BLOCK_EDGE_UNITS,
        height_extent // BLOCK_EDGE_UNITS,
        BLOCK_EDGE_UNITS,
    )
    patch_cubes = patch_cubes.transpose(0, 2, 4, 6, 1, 3, 5, 7).reshape(
        -1, CH * BLOCK_EDGE_UNITS**3
    )
    encoded = jnp.dot(patch_cubes, patch_weight, preferred_element_type=jnp.float32).reshape(
        local_frames, -1, D
    )
    time_emb, frequency = embed_time(frame_index)
    place_x = tile_place * stride_along_x + jnp.arange(stride_along_x)
    space_emb = embed_space(
        tile_offset,
        place_x,
        jnp.arange(cells_in_depth // BLOCK_EDGE_UNITS),
        jnp.arange(height_extent // BLOCK_EDGE_UNITS),
        frequency,
    )
    tokens = (encoded + time_emb[:, None, :] + space_emb[None]).astype(jnp.bfloat16)
    token_rows = tokens.reshape(-1, D)
    normed = settle(token_rows.astype(jnp.float32)).astype(jnp.bfloat16)
    row_count = token_rows.shape[0]
    projected = jnp.dot(
        normed,
        lax.all_gather(attend_weight, "tile", axis=1, tiled=True),
        preferred_element_type=jnp.float32,
    ).astype(jnp.bfloat16)
    cube_count = row_count // local_frames
    projected = projected.reshape(local_frames, cube_count, 3, HEADS, HD)
    keys_values = lax.all_gather(projected[:, :, 1:], "tm", axis=0, tiled=True)
    attended = attend_frames(
        projected[:, :, 0],
        keys_values[:, :, 0],
        keys_values[:, :, 1],
        lax.axis_index("tm") * local_frames,
    )
    attended_rows = attended.reshape(row_count, D)
    mixed_terms = jnp.dot(
        attended_rows,
        lax.all_gather(mixing_weight, "tile", axis=1, tiled=True),
        preferred_element_type=jnp.float32,
    )
    residual = token_rows.astype(jnp.float32) + mixed_terms
    ending_entries = settle(residual).astype(jnp.bfloat16)
    prediction_tensor = jnp.dot(
        ending_entries, cube_output_projector, preferred_element_type=jnp.float32
    ).astype(jnp.bfloat16)
    return prediction_tensor.reshape(
        local_frames,
        stride_along_x,
        cells_in_depth // BLOCK_EDGE_UNITS,
        height_extent // BLOCK_EDGE_UNITS,
        -1,
    )


def solution(mesh):
    placed = (
        P("tm", "tile", None, None),
        P("tm"),
        P(),
        P(),
        P(),
        P(),
        P(None, "tile"),
        P(None, "tile"),
        P(),
    )
    return jax.shard_map(
        local,
        mesh=mesh,
        in_specs=placed,
        out_specs=P("tm", "tile", None, None, None),
        check_vma=False,
    )
```

profile of v0, /device:TPU:0, one launch (start us, length us, event | category | flops | bytes accessed | tf_op | source)
XLA Modules:
  0.0 538.9 jit_solution(4593768674398260444)
XLA Ops:
  6.5 0.8 fusion.34
  7.4 3.9 collective-permute-start
  11.3 1.3 collective-permute-start.1
  12.7 1.4 fusion.35
  14.8 0.7 add_convert_fusion.1
  15.5 0.7 add_convert_fusion
  16.2 0.7 convert_element_type.69
  16.9 0.3 add_sine_fusion
  17.2 0.2 sine_add_fusion
  17.4 0.7 broadcast_add_fusion
  18.0 0.8 add_sine_fusion.1
  18.8 0.9 maximum_bitcast_fusion.1
  19.8 0.2 pad
  19.9 0.9 reshape.256
  20.9 0.4 slice.52
  21.3 0.2 copy.60
  21.5 2.0 fusion.6
  23.5 4.4 copy.19
  27.9 19.7 %multiply_convert_fusion.1 = bf16[8,16,32,17,16]{2,4,3,1,0:T(8,128)(2,1)} fusion(pred[32,17]{0,1:T(8,128)(4,1)S(1)} %copy-done.7, bf16[1,10,16,32,19]{3,0,4,2,1:T(2,128)(2,1)S(1)} %copy.19, bf16[16,1,3,3,3]{0,4,3,2,1:T(4,128)(2,1)S(1)} %copy-done.6), kind=kOutput, calls=%fused_computation.5 | convolution fusion | flops 64339968 | bytes 2424192 | tf_op jit(solution)/shard_map/conv_general_dilated | solution.py:32
  47.7 24.2 %copy.22 = bf16[8,16,32,17,16]{3,2,4,1,0:T(8,128)(2,1)} copy(bf16[8,16,32,17,16]{2,4,3,1,0:T(8,128)(2,1)} %multiply_convert_fusion.1) | data formatting | bytes 4456448 | tf_op jit(solution)/shard_map/convert_element_type | solution.py:95
  71.8 3.6 fusion.33
  75.4 3.6 copy.21
  79.0 2.3 reshape.260
  81.3 1.8 slice_bitcast_fusion.5
  83.1 4.3 collective-permute-start.2
  87.4 3.6 copy.23
  91.0 2.3 reshape.262
  93.3 1.1 slice_bitcast_fusion.4
  94.4 1.3 collective-permute-start.3
  95.7 21.7 %reshape.271 = bf16[8,16,4,136,16]{3,2,4,1,0:T(4,128)(2,1)} reshape(bf16[8,16,32,17,16]{3,2,4,1,0:T(8,128)(2,1)} %copy.22) | data formatting | bytes 4456448 | tf_op jit(solution)/shard_map/convert_element_type | solution.py:95
  117.4 2.6 slice_bitcast_fusion.1
  120.0 2.0 maximum_bitcast_fusion
  122.0 3.0 copy.42
  125.0 4.4 pad.2.clone
  129.4 24.7 %reshape.265 = bf16[16,10,16,4,8,17]{5,4,2,3,1,0:T(8,128)(2,1)} reshape(bf16[16,10,16,4,136]{4,2,3,1,0:T(8,128)(2,1)} %pad.2.clone) | data formatting | bytes 5570560 | tf_op jit(solution)/shard_map/conv_general_dilated | solution.py:32
  154.1 21.6 %slice.58 = bf16[16,10,16,4,7,2]{5,4,2,3,1,0:T(8,128)(2,1)} slice(bf16[16,10,16,4,8,17]{5,4,2,3,1,0:T(8,128)(2,1)} %reshape.265), slice={[0:16], [0:10], [0:16], [0:4], [1:8], [0:2]} | slice | bytes 573440 | tf_op jit(solution)/shard_map/conv_general_dilated | solution.py:32
  175.7 21.9 %copy_bitcast_fusion = bf16[16,10,16,32,19]{4,3,2,1,0:T(8,128)(2,1)} fusion(bf16[16,10,16,4,7,2]{5,4,2,3,1,0:T(8,128)(2,1)} %slice.58, bf16[16,10,16,4,8,17]{5,4,2,3,1,0:T(8,128)(2,1)S(1)} %copy-done.1), kind=kLoop, calls=%fused_computation.3 | loop fusion | flops 9338880 | bytes 6184960 | tf_op jit(solution)/shard_map/conv_general_dilated | solution.py:32
  197.7 28.3 %copy.26 = bf16[16,10,16,32,19]{3,0,4,2,1:T(8,128)(2,1)} copy(bf16[16,10,16,32,19]{4,3,2,1,0:T(8,128)(2,1)} %copy_bitcast_fusion) | data formatting | bytes 6225920 | tf_op jit(solution)/shard_map/conv_general_dilated | solution.py:32
  225.9 35.9 %multiply_convert_fusion = bf16[8,16,32,17,16]{2,4,3,1,0:T(8,128)(2,1)} fusion(bf16[16,10,16,32,19]{3,0,4,2,1:T(8,128)(2,1)} %copy.26, bf16[16,16,3,3,3]{1,0,4,3,2:T(8,128)(2,1)S(1)} %copy-done.5, pred[32,17]{0,1:T(8,128)(4,1)S(1)} %copy-done.7), kind=kOutput, calls=%fused_computation.4 | convolution fusion | flops 929169408 | bytes 5355552 | tf_op jit(solution)/shard_map/conv_general_dilated | solution.py:32
  261.9 24.1 %copy.27 = bf16[8,16,32,17,16]{3,2,4,1,0:T(8,128)(2,1)} copy(bf16[8,16,32,17,16]{2,4,3,1,0:T(8,128)(2,1)} %multiply_convert_fusion) | data formatting | bytes 4456448 | tf_op jit(solution)/shard_map/convert_element_type | solution.py:97
  286.0 21.3 %reshape.269 = bf16[8,16,4,136,16]{3,2,4,1,0:T(4,128)(2,1)} reshape(bf16[8,16,32,17,16]{3,2,4,1,0:T(8,128)(2,1)} %copy.27) | data formatting | bytes 4456448 | tf_op jit(solution)/shard_map/convert_element_type | solution.py:97
  307.3 2.6 slice_bitcast_fusion
  309.9 11.0 %copy.28 = bf16[4,16,8,16,128]{1,4,3,2,0:T(8,128)(2,1)} copy(bf16[4,16,8,16,128]{4,0,1,3,2:T(4,128)(2,1)S(1)} %slice_bitcast_fusion) | data formatting | bytes 4194304 | tf_op jit(solution)/shard_map/convert_element_type | solution.py:97
  320.9 51.2 %copy.29 = bf16[4,1,2,16,16,8,8,8]{3,2,7,6,5,4,0,1:T(2,128)(2,1)} copy(bf16[4,1,2,16,16,8,8,8]{4,7,3,6,2,5,0,1:T(8,128)(2,1)} %bitcast.117) | data formatting | bytes 4194304 | tf_op jit(solution)/shard_map/transpose | solution.py:109
  372.2 27.0 %dot_general.20 = bf16[4,32,8192]{1,2,0:T(8,128)(2,1)} reshape(bf16[4,1,2,16,16,8,8,8]{3,2,7,6,5,4,0,1:T(2,128)(2,1)} %copy.29) | data formatting | bytes 4194304 | tf_op jit(solution)/shard_map/dot_general | solution.py:112
  399.2 11.8 %multiply_reduce_fusion.1 = (f32[4,32]{1,0:T(4,128)S(1)}, f32[4,32,1024]{2,1,0:T(8,128)S(1)}) fusion(f32[32,1024]{1,0:T(8,128)S(1)} %bitcast.123, f32[4,1024]{1,0:T(4,128)S(1)} %copy-done.4, bf16[4,32,8192]{1,2,0:T(8,128)(2,1)} %dot_general.20, bf16[8192,1024]{1,0:T(8,128)(2,1)} %param.14), kind=kOutput, calls=%fused_computation.35 | convolution fusion | flops 2148270080 | bytes 19546624 | tf_op jit(solution)/shard_map/dot_general | solution.py:112
  411.0 0.1 rsqrt.20
  411.1 0.1 fusion.22
  411.2 5.0 fusion.7
  416.2 0.2 copy.43
  416.4 0.9 copy.40
  417.4 0.7 all-gather.8.cloned.1.call-update
  418.2 0.1 iota_compare_fusion.2
  418.2 0.1 broadcast_in_dim.23
  418.3 0.1 broadcast_in_dim.24
  418.5 35.0 %all-gather.6.cloned.1.call-done = bf16[16,32,2,8,128]{4,1,0,3,2:T(8,128)(2,1)} async-done(((bf16[4,32,2,8,128]{4,1,0,3,2:T(8,128)(2,1)}), bf16[16,32,2,8,128]{4,1,0,3,2:T(8,128)(2,1)}) %all-gather.6.cloned.1.call-update) | async-done | bytes 2097168 | tf_op jit(solution)/shard_map/all_gather | solution.py:135
  453.5 6.2 %select_reduce_fusion = (f32[8,4,32]{2,1,0:T(4,128)S(1)}, f32[8,4,32,16,32]{2,4,3,1,0:T(8,128)}) fusion(pred[4,16]{1,0:T(4,128)(4,1)S(1)} %iota_compare_fusion.2, bf16[16,32,2,8,128]{4,1,0,3,2:T(8,128)(2,1)} %all-gather.6.cloned.1.call-done, bf16[4,32,1,8,128]{4,3,2,1,0:T(8,128)(2,1)S(1)} %slice.62), kind=kOutput, calls=%fused_computation.9 | convolution fusion | flops 135789568 | bytes 3412032 | tf_op jit(solution)/shard_map/tnhd,smhd->htnsm/dot_general | solution.py:65
  459.6 6.3 %copy.33 = f32[8,4,32,512]{3,2,1,0:T(8,128)} copy(f32[8,4,32,512]{2,3,1,0:T(8,128)} %bitcast.116) | data formatting | bytes 4194304 | tf_op jit(solution)/shard_map/reshape | solution.py:68
  465.9 4.6 exponential_reduce_fusion
  470.6 0.6 fusion.20
  471.2 0.2 copy.34
  471.4 57.2 %all-gather.8.cloned.1.call-done = bf16[1024,1024]{0,1:T(8,128)(2,1)} async-done(((bf16[1024,32]{0,1:T(8,128)(2,1)}), bf16[1024,1024]{0,1:T(8,128)(2,1)}) %all-gather.8.cloned.1.call-update) | async-done | bytes 2097168 | tf_op jit(solution)/shard_map/all_gather | solution.py:145
  528.6 2.5 multiply_reduce_fusion
  531.1 1.0 convolution_convert_fusion.2
  (35 shorter events, 0.3 us)
Async XLA Ops:
  6.5 524.6 %copy-start = (bf16[1024,512]{1,0:T(8,128)(2,1)S(1)}, bf16[1024,512]{1,0:T(8,128)(2,1)}, u32[]{:S(2)}) copy-start(bf16[1024,512]{1,0:T(8,128)(2,1)} %param.17) | copy-start | bytes 3145732
  6.5 404.7 %all-gather.4.cloned.1.call-start = ((), (), s32[]{:S(2)}) async-start(), calls=%async_computation | async-start | bytes 6488064 | tf_op jit(solution)/shard_map/all_gather | solution.py:130
  7.4 11.5 %collective-permute-start = (bf16[4,1,16,128]{3,2,1,0:T(8,128)(2,1)S(1)}, bf16[4,1,16,128]{3,2,1,0:T(8,128)(2,1)S(1)}, u32[]{:S(2)}, u32[]{:S(2)}) collective-permute-start(bf16[4,1,16,128]{3,2,1,0:T(8,128)(2,1)S(1)} %get-tuple-element.7), channel_id=1, source_target_pairs={{0,4},{4,8},{8,12},{12,16},{16,20},{20,24},{24,28},{28,32},{32,36}... | collective-permute-start | bytes 49160 | tf_op jit(solution)/shard_map/ppermute | solution.py:22
  11.3 7.6 %collective-permute-start.1 = (bf16[4,1,16,128]{3,2,1,0:T(8,128)(2,1)S(1)}, bf16[4,1,16,128]{3,2,1,0:T(8,128)(2,1)S(1)}, u32[]{:S(2)}, u32[]{:S(2)}) collective-permute-start(bf16[4,1,16,128]{3,2,1,0:T(8,128)(2,1)S(1)} %get-tuple-element.8), channel_id=1, source_target_pairs={{4,0},{8,4},{12,8},{16,12},{20,16},{24,20},{28,24},{32,28},{36,32}... | collective-permute-start | bytes 49160 | tf_op jit(solution)/shard_map/ppermute | solution.py:24
  12.6 440.9 %all-gather.6.cloned.1.call-start = ((), (), s32[]{:S(2)}) async-start(), calls=%async_computation.1 | async-start | bytes 2621440 | tf_op jit(solution)/shard_map/all_gather | solution.py:135
  20.9 7.1 %copy-start.6 = (bf16[16,1,3,3,3]{0,4,3,2,1:T(4,128)(2,1)S(1)}, bf16[16,1,3,3,3]{0,4,3,2,1:T(4,128)(2,1)}, u32[]{:S(2)}) copy-start(bf16[16,1,3,3,3]{0,4,3,2,1:T(4,128)(2,1)} %param.12) | copy-start | bytes 2596
  20.9 7.1 %copy-start.7 = (pred[32,17]{0,1:T(8,128)(4,1)S(1)}, pred[32,17]{0,1:T(8,128)(4,1)}, u32[]{:S(2)}) copy-start(pred[32,17]{0,1:T(8,128)(4,1)} %constant.72) | copy-start | bytes 1636
  83.1 36.9 %collective-permute-start.2 = (bf16[4,16,1,16,128]{4,0,1,3,2:T(4,128)(2,1)}, bf16[4,16,1,16,128]{4,0,1,3,2:T(4,128)(2,1)S(1)}, u32[]{:S(2)}, u32[]{:S(2)}) collective-permute-start(bf16[4,16,1,16,128]{4,0,1,3,2:T(4,128)(2,1)} %slice_bitcast_fusion.5), channel_id=1, source_target_pairs={{0,4},{4,8},{8,12},{12,16},{16,20},{20,24},{24,28},{28,32},{32,36}... | collective-permute-start | bytes 786440 | tf_op jit(solution)/shard_map/ppermute | solution.py:22
  94.4 25.6 %collective-permute-start.3 = (bf16[4,16,1,16,128]{4,0,1,3,2:T(4,128)(2,1)S(1)}, bf16[4,16,1,16,128]{4,0,1,3,2:T(4,128)(2,1)S(1)}, u32[]{:S(2)}, u32[]{:S(2)}) collective-permute-start(bf16[4,16,1,16,128]{4,0,1,3,2:T(4,128)(2,1)S(1)} %slice_bitcast_fusion.4), channel_id=1, source_target_pairs={{4,0},{8,4},{12,8},{16,12},{20,16},{24,20},{28,24},{32,28},{36,32}... | collective-permute-start | bytes 786440 | tf_op jit(solution)/shard_map/ppermute | solution.py:24
  154.1 21.6 %copy-start.1 = (bf16[16,10,16,4,8,17]{5,4,2,3,1,0:T(8,128)(2,1)S(1)}, bf16[16,10,16,4,8,17]{5,4,2,3,1,0:T(8,128)(2,1)}, u32[]{:S(2)}) copy-start(bf16[16,10,16,4,8,17]{5,4,2,3,1,0:T(8,128)(2,1)} %reshape.265) | copy-start | bytes 8355844
  197.7 28.3 %copy-start.5 = (bf16[16,16,3,3,3]{1,0,4,3,2:T(8,128)(2,1)S(1)}, bf16[16,16,3,3,3]{1,0,4,3,2:T(8,128)(2,1)}, u32[]{:S(2)}) copy-start(bf16[16,16,3,3,3]{1,0,4,3,2:T(8,128)(2,1)} %param.13) | copy-start | bytes 41476
  372.2 27.0 %copy-start.3 = (f32[2,16,1024]{2,1,0:T(8,128)S(1)}, f32[2,16,1024]{2,1,0:T(8,128)}, u32[]{:S(2)}) copy-start(f32[2,16,1024]{2,1,0:T(8,128)} %broadcast_add_fusion) | copy-start | bytes 393220
  372.2 27.0 %copy-start.4 = (f32[4,1024]{1,0:T(4,128)S(1)}, f32[4,1024]{1,0:T(4,128)}, u32[]{:S(2)}) copy-start(f32[4,1024]{1,0:T(4,128)} %add_sine_fusion.1) | copy-start | bytes 49156
  417.4 111.2 %all-gather.8.cloned.1.call-start = ((), (), s32[]{:S(2)}) async-start(), calls=%async_computation.2 | async-start | bytes 2162688 | tf_op jit(solution)/shard_map/all_gather | solution.py:145
  465.9 4.6 copy-start.2
  465.9 4.6 slice-start
Sparse Core Ops, SparseCore 0:
  12.7 97.3 all-gather.3
  417.5 35.9 all-gather.5
  456.6 71.9 all-gather.7
where the time goes:
time: 548 us; the launch traced here: 539 us
  local copies, waits for them, and re-layouts  302 us (55%)
  waiting for transfers between devices  93 us (17%)
  matrix products  82.8 us (15%)
  other arithmetic  35.7 us (7%)
  between operations  14.3 us (3%)
  starting transfers between devices  10.9 us (2%)
    conv_general_dilated x6, local copies, waits for them, and re-layouts, convolve_strip(): lax.conv_general_dilated(field_in, kernel, (1, 1, 1), ((0, 0), (1, 1), (1...  80.3 us
    convert_element_type x8, local copies, waits for them, and re-layouts, local(): jax.nn.silu(convolve_strip(padded[:, None], conv_first))  63.9 us
    convert_element_type x4, local copies, waits for them, and re-layouts, local(): jax.nn.silu(convolve_strip(first_maps, conv_second)).astype(jnp.bfloat16)  59 us
    all_gather x1, waiting for transfers between devices, local(): lax.all_gather(mixing_weight, 'tile', axis=1, tiled=True)  57.2 us
    conv_general_dilated x2, matrix products, convolve_strip(): lax.conv_general_dilated(field_in, kernel, (1, 1, 1), ((0, 0), (1, 1), (1...  55.7 us
    transpose x1, local copies, waits for them, and re-layouts, local(): patch_cubes.transpose(0, 2, 4, 6, 1, 3, 5, 7)  51.2 us
    all_gather x1, waiting for transfers between devices, local(): keys_values = lax.all_gather(projected[:, :, 1:], 'tm', axis=0, tiled=True)  35 us
    dot_general x1, local copies, waits for them, and re-layouts, local(): jnp.dot(patch_cubes, patch_weight, preferred_element_type=jnp.float32)  27 us
  transfers between devices with their start and end apart: 7, of which 2 were waited for; matrix products, arithmetic and copies ran while one was open for 76% of the time, Pallas kernels for 0%

commit v1 on v0

--- a/solution.py
+++ b/solution.py
@@ -132,7 +132,9 @@
     ).astype(jnp.bfloat16)
     cube_count = row_count // local_frames
     projected = projected.reshape(local_frames, cube_count, 3, HEADS, HD)
-    keys_values = lax.all_gather(projected[:, :, 1:], "tm", axis=0, tiled=True)
+    keys_values = jnp.concatenate(
+        lax.all_to_all(jnp.stack([projected[:, :, 1:]] * lax.axis_size("tm")), "tm", 0, 0), axis=0
+    )
     attended = attend_frames(
         projected[:, :, 0],
         keys_values[:, :, 0],

time: 548 us -> 496 us (0.905)
  the two profiles are of different devices: /device:TPU:0 before, /device:TPU:6 now
where the time goes in v1:
time: 496 us; the launch traced here: 487 us
  local copies, waits for them, and re-layouts  307 us (62%)
  matrix products  79.4 us (16%)
  other arithmetic  35.6 us (7%)
  waiting for transfers between devices  25.2 us (5%)
  starting transfers between devices  24.8 us (5%)
  between operations  14.6 us (3%)
    conv_general_dilated x6, local copies, waits for them, and re-layouts, convolve_strip(): lax.conv_general_dilated(field_in, kernel, (1, 1, 1), ((0, 0), (1, 1), (1...  80.3 us
    convert_element_type x8, local copies, waits for them, and re-layouts, local(): jax.nn.silu(convolve_strip(padded[:, None], conv_first))  61.9 us
    convert_element_type x4, local copies, waits for them, and re-layouts, local(): jax.nn.silu(convolve_strip(first_maps, conv_second)).astype(jnp.bfloat16)  59 us
    conv_general_dilated x2, matrix products, convolve_strip(): lax.conv_general_dilated(field_in, kernel, (1, 1, 1), ((0, 0), (1, 1), (1...  53.5 us
    transpose x1, local copies, waits for them, and re-layouts, local(): patch_cubes.transpose(0, 2, 4, 6, 1, 3, 5, 7)  51.2 us
    dot_general x1, local copies, waits for them, and re-layouts, local(): jnp.dot(patch_cubes, patch_weight, preferred_element_type=jnp.float32)  27 us
    all_to_all x1, waiting for transfers between devices, local(): lax.all_to_all(jnp.stack([projected[:, :, 1:]] * lax.axis_size('tm')), 't...  24.4 us
    conv_general_dilated x2, other arithmetic, convolve_strip(): lax.conv_general_dilated(field_in, kernel, (1, 1, 1), ((0, 0), (1, 1), (1...  23.9 us
  transfers between devices with their start and end apart: 7, of which 1 were waited for; matrix products, arithmetic and copies ran while one was open for 85% of the time, Pallas kernels for 0%

profile of v1, /device:TPU:6, one launch (start us, length us, event | category | flops | bytes accessed | tf_op | source)
XLA Modules:
  0.0 486.7 jit_solution(13549388040641826613)
XLA Ops:
  6.5 0.7 all-gather.3.cloned.1.call-update
  7.3 0.7 fusion.34
  8.1 3.8 collective-permute-start
  11.9 6.9 %collective-permute-start.1 = (bf16[4,1,16,128]{3,2,1,0:T(8,128)(2,1)S(1)}, bf16[4,1,16,128]{3,2,1,0:T(8,128)(2,1)S(1)}, u32[]{:S(2)}, u32[]{:S(2)}) collective-permute-start(bf16[4,1,16,128]{3,2,1,0:T(8,128)(2,1)S(1)} %get-tuple-element.8), channel_id=1, source_target_pairs={{4,0},{8,4},{12,8},{16,12},{20,16},{24,20},{28,24},{32,28},{36,32}... | collective-permute-start | bytes 49160 | tf_op jit(solution)/shard_map/ppermute | solution.py:24
  18.9 1.4 fusion.35
  20.9 0.7 add_convert_fusion.1
  21.6 0.7 add_convert_fusion
  22.3 0.7 convert_element_type.69
  22.9 0.3 add_sine_fusion
  23.2 0.2 sine_add_fusion
  23.4 0.7 broadcast_add_fusion
  24.1 0.8 add_sine_fusion.1
  24.9 0.9 maximum_bitcast_fusion.1
  25.8 0.2 pad
  26.0 0.9 reshape.262
  26.9 0.4 slice.52
  27.3 0.2 copy.79
  27.6 2.0 fusion.6
  29.6 4.4 copy.38
  34.0 17.6 %multiply_convert_fusion.1 = bf16[8,16,32,17,16]{2,4,3,1,0:T(8,128)(2,1)S(1)} fusion(pred[32,17]{0,1:T(8,128)(4,1)S(1)} %copy-done.11, bf16[1,10,16,32,19]{3,0,4,2,1:T(2,128)(2,1)S(1)} %copy.38, bf16[16,1,3,3,3]{0,4,3,2,1:T(4,128)(2,1)S(1)} %copy-done.10), kind=kOutput, calls=%fused_computation.5 | convolution fusion | flops 64339968 | bytes 2424192 | tf_op jit(solution)/shard_map/conv_general_dilated | solution.py:32
  51.6 3.4 copy-done.2
  55.0 1.8 fusion.33
  56.8 24.2 %copy.41 = bf16[8,16,32,17,16]{3,2,4,1,0:T(8,128)(2,1)} copy(bf16[8,16,32,17,16]{2,4,3,1,0:T(8,128)(2,1)} %copy-done.2) | data formatting | bytes 4456448 | tf_op jit(solution)/shard_map/convert_element_type | solution.py:95
  81.0 3.6 copy.40
  84.6 2.3 reshape.266
  86.9 1.8 slice_bitcast_fusion.5
  88.7 1.9 collective-permute-start.2
  90.6 3.6 copy.42
  94.2 2.3 reshape.268
  96.5 1.0 slice_bitcast_fusion.4
  97.6 8.5 %collective-permute-start.3 = (bf16[4,16,1,16,128]{4,0,1,3,2:T(4,128)(2,1)S(1)}, bf16[4,16,1,16,128]{4,0,1,3,2:T(4,128)(2,1)S(1)}, u32[]{:S(2)}, u32[]{:S(2)}) collective-permute-start(bf16[4,16,1,16,128]{4,0,1,3,2:T(4,128)(2,1)S(1)} %slice_bitcast_fusion.4), channel_id=1, source_target_pairs={{4,0},{8,4},{12,8},{16,12},{20,16},{24,20},{28,24},{32,28},{36,32}... | collective-permute-start | bytes 786440 | tf_op jit(solution)/shard_map/ppermute | solution.py:24
  106.0 21.6 %reshape.277 = bf16[8,16,4,136,16]{3,2,4,1,0:T(4,128)(2,1)} reshape(bf16[8,16,32,17,16]{3,2,4,1,0:T(8,128)(2,1)} %copy.41) | data formatting | bytes 4456448 | tf_op jit(solution)/shard_map/convert_element_type | solution.py:95
  127.6 2.6 slice_bitcast_fusion.1
  130.2 2.0 maximum_bitcast_fusion
  132.2 3.0 copy.61
  135.3 4.4 pad.2.clone
  139.7 24.7 %reshape.271 = bf16[16,10,16,4,8,17]{5,4,2,3,1,0:T(8,128)(2,1)} reshape(bf16[16,10,16,4,136]{4,2,3,1,0:T(8,128)(2,1)} %pad.2.clone) | data formatting | bytes 5570560 | tf_op jit(solution)/shard_map/conv_general_dilated | solution.py:32
  164.3 21.7 %slice.58 = bf16[16,10,16,4,7,2]{5,4,2,3,1,0:T(8,128)(2,1)} slice(bf16[16,10,16,4,8,17]{5,4,2,3,1,0:T(8,128)(2,1)} %reshape.271), slice={[0:16], [0:10], [0:16], [0:4], [1:8], [0:2]} | slice | bytes 573440 | tf_op jit(solution)/shard_map/conv_general_dilated | solution.py:32
  186.1 21.9 %copy_bitcast_fusion = bf16[16,10,16,32,19]{4,3,2,1,0:T(8,128)(2,1)} fusion(bf16[16,10,16,4,7,2]{5,4,2,3,1,0:T(8,128)(2,1)} %slice.58, bf16[16,10,16,4,8,17]{5,4,2,3,1,0:T(8,128)(2,1)S(1)} %copy-done.1), kind=kLoop, calls=%fused_computation.3 | loop fusion | flops 9338880 | bytes 6184960 | tf_op jit(solution)/shard_map/conv_general_dilated | solution.py:32
  208.0 28.2 %copy.45 = bf16[16,10,16,32,19]{3,0,4,2,1:T(8,128)(2,1)} copy(bf16[16,10,16,32,19]{4,3,2,1,0:T(8,128)(2,1)} %copy_bitcast_fusion) | data formatting | bytes 6225920 | tf_op jit(solution)/shard_map/conv_general_dilated | solution.py:32
  236.2 35.9 %multiply_convert_fusion = bf16[8,16,32,17,16]{2,4,3,1,0:T(8,128)(2,1)} fusion(bf16[16,10,16,32,19]{3,0,4,2,1:T(8,128)(2,1)} %copy.45, bf16[16,16,3,3,3]{1,0,4,3,2:T(8,128)(2,1)S(1)} %copy-done.9, pred[32,17]{0,1:T(8,128)(4,1)S(1)} %copy-done.11), kind=kOutput, calls=%fused_computation.4 | convolution fusion | flops 929169408 | bytes 5355552 | tf_op jit(solution)/shard_map/conv_general_dilated | solution.py:32
  272.2 24.1 %copy.46 = bf16[8,16,32,17,16]{3,2,4,1,0:T(8,128)(2,1)} copy(bf16[8,16,32,17,16]{2,4,3,1,0:T(8,128)(2,1)} %multiply_convert_fusion) | data formatting | bytes 4456448 | tf_op jit(solution)/shard_map/convert_element_type | solution.py:97
  296.3 21.3 %reshape.275 = bf16[8,16,4,136,16]{3,2,4,1,0:T(4,128)(2,1)} reshape(bf16[8,16,32,17,16]{3,2,4,1,0:T(8,128)(2,1)} %copy.46) | data formatting | bytes 4456448 | tf_op jit(solution)/shard_map/convert_element_type | solution.py:97
  317.6 2.6 slice_bitcast_fusion
  320.2 11.0 %copy.47 = bf16[4,16,8,16,128]{1,4,3,2,0:T(8,128)(2,1)} copy(bf16[4,16,8,16,128]{4,0,1,3,2:T(4,128)(2,1)S(1)} %slice_bitcast_fusion) | data formatting | bytes 4194304 | tf_op jit(solution)/shard_map/convert_element_type | solution.py:97
  331.2 51.2 %copy.48 = bf16[4,1,2,16,16,8,8,8]{3,2,7,6,5,4,0,1:T(2,128)(2,1)} copy(bf16[4,1,2,16,16,8,8,8]{4,7,3,6,2,5,0,1:T(8,128)(2,1)} %bitcast.118) | data formatting | bytes 4194304 | tf_op jit(solution)/shard_map/transpose | solution.py:109
  382.5 27.0 %dot_general.20 = bf16[4,32,8192]{1,2,0:T(8,128)(2,1)} reshape(bf16[4,1,2,16,16,8,8,8]{3,2,7,6,5,4,0,1:T(2,128)(2,1)} %copy.48) | data formatting | bytes 4194304 | tf_op jit(solution)/shard_map/dot_general | solution.py:112
  409.5 11.8 %multiply_reduce_fusion.1 = (f32[4,32]{1,0:T(4,128)S(1)}, f32[4,32,1024]{2,1,0:T(8,128)S(1)}) fusion(f32[32,1024]{1,0:T(8,128)S(1)} %bitcast.126, f32[4,1024]{1,0:T(4,128)S(1)} %copy-done.8, bf16[4,32,8192]{1,2,0:T(8,128)(2,1)} %dot_general.20, bf16[8192,1024]{1,0:T(8,128)(2,1)} %param.14), kind=kOutput, calls=%fused_computation.35 | convolution fusion | flops 2148270080 | bytes 19546624 | tf_op jit(solution)/shard_map/dot_general | solution.py:112
  421.5 5.0 %fusion.7 = bf16[16,8,24,128]{3,1,2,0:T(8,128)(2,1)S(1)} fusion(bf16[128,1024]{1,0:T(8,128)(2,1)S(1)} %fusion.22, bf16[1024,3072]{0,1:T(8,128)(2,1)} %all-gather.3.cloned.1.call-done), kind=kOutput, calls=%fused_computation.20 | convolution fusion | flops 805699584 | bytes 7340032 | tf_op jit(solution)/shard_map/dot_general | solution.py:128
  426.5 0.2 copy.62
  426.7 0.9 copy-done.5
  427.7 1.9 stack.2
  429.6 3.6 all-to-all-start
  433.5 1.0 slice.62
  434.4 24.4 %all-to-all-done = bf16[4,4,32,2,8,128]{5,2,1,4,3,0:T(8,128)(2,1)S(1)} async-done(((bf16[4,4,32,2,8,128]{5,2,1,4,3,0:T(8,128)(2,1)}), bf16[4,4,32,2,8,128]{5,2,1,4,3,0:T(8,128)(2,1)S(1)}, u32[]{:S(2)}, u32[]{:S(2)}) %all-to-all-start) | async-done | bytes 2097184 | tf_op jit(solution)/shard_map/all_to_all | solution.py:136
  458.9 0.4 copy.51
  459.3 5.0 %select_reduce_fusion = (f32[8,4,32]{2,1,0:T(4,128)S(1)}, f32[8,4,32,16,32]{2,4,3,1,0:T(8,128)}) fusion(pred[4,16]{1,0:T(4,128)(4,1)S(1)} %iota_compare_fusion.2, bf16[16,32,2,8,128]{4,1,0,3,2:T(8,128)(2,1)S(1)} %bitcast.120, bf16[4,32,1,8,128]{4,3,2,1,0:T(8,128)(2,1)S(1)} %slice.62), kind=kOutput, calls=%fused_computation.9 | convolution fusion | flops 135789568 | bytes 3412480 | tf_op jit(solution)/shard_map/tnhd,smhd->htnsm/dot_general | solution.py:65
  464.3 6.3 %copy.53 = f32[8,4,32,512]{3,2,1,0:T(8,128)} copy(f32[8,4,32,512]{2,3,1,0:T(8,128)} %bitcast.117) | data formatting | bytes 4194304 | tf_op jit(solution)/shard_map/reshape | solution.py:68
  470.6 4.5 exponential_reduce_fusion
  475.1 0.6 fusion.20
  475.8 0.2 copy.54
  476.0 0.2 copy-done.4
  476.1 2.5 multiply_reduce_fusion
  478.7 1.0 convolution_convert_fusion.2
  (43 shorter events, 0.9 us)
Async XLA Ops:
  6.5 472.1 %copy-start = (bf16[1024,512]{1,0:T(8,128)(2,1)S(1)}, bf16[1024,512]{1,0:T(8,128)(2,1)}, u32[]{:S(2)}) copy-start(bf16[1024,512]{1,0:T(8,128)(2,1)} %param.17) | copy-start | bytes 3145732
  6.5 414.9 %all-gather.3.cloned.1.call-start = ((), (), s32[]{:S(2)}) async-start(), calls=%async_computation.1 | async-start | bytes 6488064 | tf_op jit(solution)/shard_map/all_gather | solution.py:130
  7.3 468.7 %all-gather.5.cloned.1.call-start = ((), (), s32[]{:S(2)}) async-start(), calls=%async_computation.2 | async-start | bytes 2162688 | tf_op jit(solution)/shard_map/all_gather | solution.py:147
  8.1 16.8 %collective-permute-start = (bf16[4,1,16,128]{3,2,1,0:T(8,128)(2,1)S(1)}, bf16[4,1,16,128]{3,2,1,0:T(8,128)(2,1)S(1)}, u32[]{:S(2)}, u32[]{:S(2)}) collective-permute-start(bf16[4,1,16,128]{3,2,1,0:T(8,128)(2,1)S(1)} %get-tuple-element.7), channel_id=1, source_target_pairs={{0,4},{4,8},{8,12},{12,16},{16,20},{20,24},{24,28},{28,32},{32,36}... | collective-permute-start | bytes 49160 | tf_op jit(solution)/shard_map/ppermute | solution.py:22
  11.9 13.0 %collective-permute-start.1 = (bf16[4,1,16,128]{3,2,1,0:T(8,128)(2,1)S(1)}, bf16[4,1,16,128]{3,2,1,0:T(8,128)(2,1)S(1)}, u32[]{:S(2)}, u32[]{:S(2)}) collective-permute-start(bf16[4,1,16,128]{3,2,1,0:T(8,128)(2,1)S(1)} %get-tuple-element.8), channel_id=1, source_target_pairs={{4,0},{8,4},{12,8},{16,12},{20,16},{24,20},{28,24},{32,28},{36,32}... | collective-permute-start | bytes 49160 | tf_op jit(solution)/shard_map/ppermute | solution.py:24
  26.9 7.0 %copy-start.10 = (bf16[16,1,3,3,3]{0,4,3,2,1:T(4,128)(2,1)S(1)}, bf16[16,1,3,3,3]{0,4,3,2,1:T(4,128)(2,1)}, u32[]{:S(2)}) copy-start(bf16[16,1,3,3,3]{0,4,3,2,1:T(4,128)(2,1)} %param.12) | copy-start | bytes 2596
  26.9 7.0 %copy-start.11 = (pred[32,17]{0,1:T(8,128)(4,1)S(1)}, pred[32,17]{0,1:T(8,128)(4,1)}, u32[]{:S(2)}) copy-start(pred[32,17]{0,1:T(8,128)(4,1)} %constant.72) | copy-start | bytes 1636
  51.6 3.4 copy-start.2
  88.7 41.5 %collective-permute-start.2 = (bf16[4,16,1,16,128]{4,0,1,3,2:T(4,128)(2,1)}, bf16[4,16,1,16,128]{4,0,1,3,2:T(4,128)(2,1)S(1)}, u32[]{:S(2)}, u32[]{:S(2)}) collective-permute-start(bf16[4,16,1,16,128]{4,0,1,3,2:T(4,128)(2,1)} %slice_bitcast_fusion.5), channel_id=1, source_target_pairs={{0,4},{4,8},{8,12},{12,16},{16,20},{20,24},{24,28},{28,32},{32,36}... | collective-permute-start | bytes 786440 | tf_op jit(solution)/shard_map/ppermute | solution.py:22
  97.6 32.6 %collective-permute-start.3 = (bf16[4,16,1,16,128]{4,0,1,3,2:T(4,128)(2,1)S(1)}, bf16[4,16,1,16,128]{4,0,1,3,2:T(4,128)(2,1)S(1)}, u32[]{:S(2)}, u32[]{:S(2)}) collective-permute-start(bf16[4,16,1,16,128]{4,0,1,3,2:T(4,128)(2,1)S(1)} %slice_bitcast_fusion.4), channel_id=1, source_target_pairs={{4,0},{8,4},{12,8},{16,12},{20,16},{24,20},{28,24},{32,28},{36,32}... | collective-permute-start | bytes 786440 | tf_op jit(solution)/shard_map/ppermute | solution.py:24
  164.3 21.7 %copy-start.1 = (bf16[16,10,16,4,8,17]{5,4,2,3,1,0:T(8,128)(2,1)S(1)}, bf16[16,10,16,4,8,17]{5,4,2,3,1,0:T(8,128)(2,1)}, u32[]{:S(2)}) copy-start(bf16[16,10,16,4,8,17]{5,4,2,3,1,0:T(8,128)(2,1)} %reshape.271) | copy-start | bytes 8355844
  208.0 28.3 %copy-start.9 = (bf16[16,16,3,3,3]{1,0,4,3,2:T(8,128)(2,1)S(1)}, bf16[16,16,3,3,3]{1,0,4,3,2:T(8,128)(2,1)}, u32[]{:S(2)}) copy-start(bf16[16,16,3,3,3]{1,0,4,3,2:T(8,128)(2,1)} %param.13) | copy-start | bytes 41476
  382.4 27.0 %copy-start.7 = (f32[2,16,1024]{2,1,0:T(8,128)S(1)}, f32[2,16,1024]{2,1,0:T(8,128)}, u32[]{:S(2)}) copy-start(f32[2,16,1024]{2,1,0:T(8,128)} %broadcast_add_fusion) | copy-start | bytes 393220
  382.4 27.0 %copy-start.8 = (f32[4,1024]{1,0:T(4,128)S(1)}, f32[4,1024]{1,0:T(4,128)}, u32[]{:S(2)}) copy-start(f32[4,1024]{1,0:T(4,128)} %add_sine_fusion.1) | copy-start | bytes 49156
  421.3 8.3 %copy-start.3 = (f32[4,32,1024]{2,1,0:T(8,128)}, f32[4,32,1024]{2,1,0:T(8,128)S(1)}, u32[]{:S(2)}) copy-start(f32[4,32,1024]{2,1,0:T(8,128)S(1)} %get-tuple-element.13) | copy-start | bytes 1572868
  426.7 0.9 copy-start.5
  429.6 29.3 %all-to-all-start = ((bf16[4,4,32,2,8,128]{5,2,1,4,3,0:T(8,128)(2,1)}), bf16[4,4,32,2,8,128]{5,2,1,4,3,0:T(8,128)(2,1)S(1)}, u32[]{:S(2)}, u32[]{:S(2)}) async-start(bf16[4,4,32,2,8,128]{5,2,1,4,3,0:T(8,128)(2,1)} %stack.2), calls=%async_computation | async-start | bytes 4194304 | tf_op jit(solution)/shard_map/all_to_all | solution.py:136
  470.6 4.6 copy-start.6
  475.1 1.0 copy-start.4
Sparse Core Ops, SparseCore 0:
  10.4 98.9 all-gather.2
  112.5 65.5 all-gather.4
